TPU v7x, 32 devices: a whole 2x2x4 slice. The times are simulated.
32 devices in a mesh: rep: 4 (over x, core), dp: 8 (over z, y).
Axes of the slice: x: 2, y: 2, z: 4, core: 2. Of those that a mesh axis runs over, the one named last changes fastest.
Arguments:
- hidden: bfloat16 [2, 4, 4096, 1920], P(None, 'rep', 'dp'), may hold values from -6 to 6
- partners: int32 [2, 4], replicated, may hold values from 0 to 3, as said below
- frame_mask: int32 [2, 4096], P(None, 'dp'), may hold values 0 or 1
- segment_ids: int32 [2, 4096], P(None, 'dp'), may hold values from 0 to 7, as said below
- master: float32 [4, 1920, 500], P('rep', 'dp'), may hold values from -0.125 to 0.125
- moment_one: float32 [4, 1920, 500], P('rep', 'dp'), may hold values from -3 to 3
- moment_two: float32 [4, 1920, 500], P('rep', 'dp'), may hold values from 0.1 to 10
Outputs:
- hidden_grad: bfloat16 [2, 4, 4096, 1920], P(None, 'rep', 'dp')
- new_master: float32 [4, 1920, 500], P('rep', 'dp')
- new_moment_one: float32 [4, 1920, 500], P('rep', 'dp')
- new_moment_two: float32 [4, 1920, 500], P('rep', 'dp')
Inputs may be any that keep to these rules, and one draw needn't show every extreme that they name: `partners`: each row is a permutation of the replicas forming one cycle through all of them, so no replica is its own partner. `segment_ids`: within each aligned block of 512 frames the ids start at 0 and never fall.
All inputs are finite; a program needn't handle non-finite values. No bound on the sum of `frame_mask` on one device may be relied on, other than what follows from the above.
Results may differ from a plain program's by a relative error of at most 0.035.
Values may be sent and summed in bfloat16 or wider, within the bound.
No kernel may reach another device: no remote copies, remote signals or barrier semaphores. Data moves between devices by JAX's collectives and lax.ppermute only.
A program may use at most 64 MiB of HBM per device.

v0:
```python
import jax
import jax.numpy as jnp
from jax import lax
from jax.sharding import PartitionSpec as P

SEGS = 8


def per_device(hidden, partners, frame_mask, segment_ids, master, moment_one, moment_two):
    frame_count = hidden.shape[2]
    feature_dim = hidden.shape[3]
    head_low = master.astype(jnp.bfloat16)
    head_full = lax.all_gather(head_low, "dp", axis=1, tiled=True)[0]
    frames_all = hidden[:, 0].reshape(2 * frame_count, feature_dim)
    logits = jnp.dot(frames_all, head_full, preferred_element_type=jnp.float32)
    logits = logits.reshape(2, frame_count, head_full.shape[1])
    sent = logits.astype(jnp.bfloat16)[None]
    mine = lax.axis_index("rep")
    partner_now = partners[:, mine]
    piece = lax.all_gather(sent, "rep", axis=0, tiled=True)
    offsets = jnp.arange(piece.shape[0], dtype=jnp.int32)
    selector = (offsets[:, None] == partner_now[None, :]).astype(jnp.bfloat16)
    other = jnp.einsum("km,kmtv->mtv", selector, piece, preferred_element_type=jnp.float32)
    valid = frame_mask.astype(jnp.float32)
    onehot = (segment_ids[..., None] == jnp.arange(SEGS, dtype=jnp.int32)).astype(jnp.float32)
    counts = jnp.sum(onehot * valid[..., None], axis=1)
    per_frame = jnp.sum(onehot * counts[:, None, :], axis=-1)
    scale = valid / jnp.maximum(per_frame, 1.0)
    grad = ((logits - other) * scale[:, :, None]).astype(jnp.bfloat16)
    grad_all = grad.reshape(2 * frame_count, grad.shape[2])
    hidden_grad = jnp.einsum("tv,dv->td", grad_all, head_full, preferred_element_type=jnp.float32)
    hidden_grad = hidden_grad.astype(jnp.bfloat16).reshape(2, 1, frame_count, feature_dim)
    head_grad = lax.psum_scatter(
        jnp.einsum("td,tv->dv", frames_all, grad_all, preferred_element_type=jnp.float32).astype(
            jnp.bfloat16
        ),
        "dp",
        scatter_dimension=0,
        tiled=True,
    ).astype(jnp.float32)
    head_grad = head_grad[None]
    new_moment_one = 0.9 * moment_one + 0.1 * head_grad
    new_moment_two = 0.99 * moment_two + 0.01 * head_grad * head_grad
    new_master = master - 0.01 * new_moment_one / (jnp.sqrt(new_moment_two) + 1e-08)
    return (hidden_grad, new_master, new_moment_one, new_moment_two)


def solution(mesh):
    placed = (
        P(None, "rep", "dp", None),
        P(),
        P(None, "dp"),
        P(None, "dp"),
        P("rep", "dp", None),
        P("rep", "dp", None),
        P("rep", "dp", None),
    )
    return jax.shard_map(
        per_device,
        mesh=mesh,
        in_specs=placed,
        out_specs=(
            P(None, "rep", "dp", None),
            P("rep", "dp", None),
            P("rep", "dp", None),
            P("rep", "dp", None),
        ),
        check_vma=False,
    )
```

profile of v0, /device:TPU:0, one launch (start us, length us, event | category | flops | bytes accessed | tf_op | source)
XLA Modules:
  0.0 191.2 jit_solution(8619591944406147875)
XLA Ops:
  7.2 1.8 convert_element_type.26
  9.0 0.0 all-gather.6.cloned.1.call-start
  9.1 52.2 %all-gather.4.cloned.1.call-done = bf16[1,1920,500]{2,1,0:T(8,128)(2,1)} async-done(((bf16[1,240,500]{2,1,0:T(8,128)(2,1)}), bf16[1,1920,500]{2,1,0:T(8,128)(2,1)}) %all-gather.4.cloned.1.call-update) | async-done | bytes 1920016 | tf_op jit(solution)/shard_map/all_gather | solution.py:13
  61.3 6.0 %fusion.20 = (bf16[2,512,500]{1,2,0:T(8,128)(2,1)}, f32[2,512,500]{1,2,0:T(8,128)S(1)}) fusion(bf16[1,1920,500]{2,1,0:T(8,128)(2,1)} %all-gather.4.cloned.1.call-done, bf16[2,1,512,1920]{3,2,1,0:T(8,128)(2,1)} %param.7), kind=kOutput, calls=%fused_computation.30 | convolution fusion | flops 1966592000 | bytes 8924160 | tf_op jit(solution)/shard_map/dot_general | solution.py:15
  67.4 0.2 dynamic-slice_reduce_fusion
  67.6 0.1 fusion.21
  67.7 32.5 %all-gather.6.cloned.1.call-done = bf16[8,512,500]{1,2,0:T(8,128)(2,1)} async-done(((bf16[2,512,500]{1,2,0:T(8,128)(2,1)}), bf16[8,512,500]{1,2,0:T(8,128)(2,1)}) %all-gather.6.cloned.1.call-update) | async-done | bytes 4096016 | tf_op jit(solution)/shard_map/all_gather | solution.py:20
  100.2 3.4 %multiply_reduce_fusion = f32[2,512,500]{1,2,0:T(8,128)S(1)} fusion(bf16[2,4,512,500]{2,3,0,1:T(8,128)(2,1)} %bitcast.43, f32[2,4]{0,1:T(4,128)S(1)} %fusion.16), kind=kLoop, calls=%fused_computation.1 | loop fusion | flops 5632000 | bytes 6144032 | tf_op jit(solution)/shard_map/km,kmtv->mtv/dot_general | solution.py:23
  103.6 0.6 multiply_convert_fusion
  104.2 1.3 copy.38
  105.5 4.8 %fusion.3 = bf16[1920,500]{0,1:T(8,128)(2,1)S(1)} fusion(bf16[1024,500]{1,0:T(8,128)(2,1)} %bitcast.44, bf16[1024,1920]{1,0:T(8,128)(2,1)} %bitcast.46), kind=kOutput, calls=%fused_computation.6 | convolution fusion | flops 1967040000 | bytes 6876160 | tf_op jit(solution)/shard_map/td,tv->dv/dot_general | solution.py:34
  110.3 2.3 %copy.52 = bf16[1920,500]{1,0:T(8,128)(2,1)} copy(bf16[1920,500]{0,1:T(8,128)(2,1)S(1)} %fusion.3) | data formatting | bytes 3840000
  112.7 0.2 copy.41
  112.9 0.8 copy-done.3
  113.7 0.2 copy.39
  113.9 0.2 copy.40
  114.1 0.1 copy-done.2
  114.2 5.8 %convolution_convert_fusion = bf16[1024,1920]{1,0:T(8,128)(2,1)} fusion(bf16[1024,500]{1,0:T(8,128)(2,1)S(1)} %bitcast.45, bf16[1,1920,500]{2,1,0:T(8,128)(2,1)} %all-gather.4.cloned.1.call-done), kind=kOutput, calls=%fused_computation.4 | convolution fusion | flops 1968046080 | bytes 6876160 | tf_op jit(solution)/shard_map/tv,dv->td/dot_general | solution.py:31
  120.0 60.3 %reduce-scatter.4.cloned.1.call-done = bf16[240,500]{1,0:T(8,128)(2,1)} async-done(((bf16[1920,500]{1,0:T(8,128)(2,1)}), bf16[240,500]{1,0:T(8,128)(2,1)}) %reduce-scatter.4.cloned.1.call-update) | async-done | bytes 240016
  180.3 1.1 copy.53
  181.4 0.4 divide_subtract_fusion
  181.7 1.0 copy.43
  182.7 1.0 copy.44
  183.7 1.0 copy.45
  (20 shorter events, 0.2 us)
Async XLA Ops:
  7.2 60.2 %copy-start = (s32[2,4]{1,0:T(2,128)S(1)}, s32[2,4]{1,0:T(2,128)}, u32[]{:S(2)}) copy-start(s32[2,4]{1,0:T(2,128)} %param.8) | copy-start | bytes 100
  7.2 54.1 %all-gather.4.cloned.1.call-start = ((), (), s32[]{:S(2)}) async-start(), calls=%async_computation.1 | async-start | bytes 2211840 | tf_op jit(solution)/shard_map/all_gather | solution.py:13
  9.0 58.4 %copy-start.5 = (s32[2,512]{1,0:T(2,128)S(1)}, s32[2,512]{1,0:T(2,128)}, u32[]{:S(2)}) copy-start(s32[2,512]{1,0:T(2,128)} %param.9) | copy-start | bytes 12292
  9.0 58.6 %copy-start.6 = (s32[2,512]{1,0:T(2,128)S(1)}, s32[2,512]{1,0:T(2,128)}, u32[]{:S(2)}) copy-start(s32[2,512]{1,0:T(2,128)} %param.10) | copy-start | bytes 12292
  9.0 91.2 %all-gather.6.cloned.1.call-start = ((), (), s32[]{:S(2)}) async-start(), calls=%async_computation.2 | async-start | bytes 5160960 | tf_op jit(solution)/shard_map/all_gather | solution.py:20
  67.3 113.0 %reduce-scatter.4.cloned.1.call-start = ((), (), s32[]{:S(2)}) async-start(), calls=%async_computation.3 | async-start | bytes 2211840
  110.3 2.4 %copy-start.1 = (f32[1,240,500]{2,1,0:T(8,128)S(1)}, f32[1,240,500]{2,1,0:T(8,128)}, u32[]{:S(2)}) copy-start(f32[1,240,500]{2,1,0:T(8,128)} %param.11) | copy-start | bytes 1440004
  112.6 1.0 copy-start.3
  112.6 1.2 copy-start.4
  112.6 1.5 copy-start.2
Sparse Core Ops, SparseCore 0:
  10.7 50.4 all-gather.3
  67.4 32.6 all-gather.5
  112.8 67.4 reduce-scatter.3
where the time goes:
time: 191 us
  waiting for transfers between devices  145 us (76%)
  matrix products  16.7 us (9%)
  between operations  13.9 us (7%)
  local copies, waits for them, and re-layouts  9.33 us (5%)
  other arithmetic  6.23 us (3%)
    unnamed x4, waiting for transfers between devices  60.3 us
    all_gather x1, waiting for transfers between devices, per_device(): head_full = lax.all_gather(head_low, 'dp', axis=1, tiled=True)[0]  52.2 us
    all_gather x1, waiting for transfers between devices, per_device(): piece = lax.all_gather(sent, 'rep', axis=0, tiled=True)  32.5 us
    unnamed x22, local copies, waits for them, and re-layouts  7.82 us
    dot_general x1, matrix products, per_device(): logits = jnp.dot(frames_all, head_full, preferred_element_type=jnp.float32)  6.04 us
    dot_general x1, matrix products, per_device(): jnp.einsum('tv,dv->td', grad_all, head_full, preferred_element_type=jnp.f...  5.85 us
    dot_general x1, matrix products, per_device(): jnp.einsum('td,tv->dv', frames_all, grad_all, preferred_element_type=jnp....  4.78 us
  transfers between devices with their start and end apart: 3, of which 3 were waited for; matrix products, arithmetic and copies ran while one was open for 4% of the time, Pallas kernels for 0%

commit v1 on v0

v1 whole, which is shorter than its diff:
```python
import jax
import jax.numpy as jnp
from jax import lax
from jax.experimental import pallas as pl
from jax.experimental.pallas import tpu as pltpu
from jax.sharding import PartitionSpec as P


SEGS = 8
LANES = 128
F32, BF16 = jnp.float32, jnp.bfloat16
VMEM = pl.BlockSpec(memory_space=pltpu.VMEM)
SMEM = pl.BlockSpec(memory_space=pltpu.SMEM)
SMALL = pltpu.CompilerParams(vmem_limit_bytes=12 << 20)


def cost(flops, nbytes):
    return pl.CostEstimate(flops=flops, bytes_accessed=nbytes, transcendentals=0)


def shape(dims, dtype):
    return jax.ShapeDtypeStruct(dims, dtype)


class Ring:
    def __init__(self, axis, n):
        order = list(range(0, n, 2)) + list(range(n - 1 - (n % 2), 0, -2))
        self.axis, self.n = axis, n
        self.up = [(order[i], order[(i + 1) % n]) for i in range(n)]
        self.down = [(b, a) for a, b in self.up]

    def owner(self, k):
        n, d = self.n, lax.axis_index(self.axis)
        place = jnp.where(d % 2 == 0, d // 2, n - 1 - d // 2)
        at = (place + k) % n
        return jnp.where(at < (n + 1) // 2, 2 * at, 2 * (n - at) - 1)

    def steps(self, up_longer):
        n = self.n
        return (n // 2, (n - 1) // 2) if up_longer else ((n - 1) // 2, n // 2)

    def send_up(self, x):
        return lax.ppermute(x, self.axis, self.up)

    def send_down(self, x):
        return lax.ppermute(x, self.axis, self.down)

    def gather(self, block, up_longer):
        ups, downs = self.steps(up_longer)
        found = {0: block}
        ahead = behind = block
        for step in range(1, max(ups, downs) + 1):
            if step <= ups:
                ahead = self.send_up(ahead)
                found[self.n - step] = ahead
            if step <= downs:
                behind = self.send_down(behind)
                found[step] = behind
        return [found[k] for k in range(self.n)]

    def scatter_sum(self, terms, up_longer):
        ups, downs = self.steps(up_longer)
        ahead = behind = None
        for step in range(max(ups, downs), 0, -1):
            if step <= ups:
                out = terms[step] if ahead is None else terms[step] + ahead
                ahead = self.send_up(out)
            if step <= downs:
                out = terms[self.n - step] if behind is None else terms[self.n - step] + behind
                behind = self.send_down(out)
        return [terms[0], ahead, behind]


def round_head(master, spans):
    def body(src, *outs):
        for (a, b), out in zip(spans, outs):
            out[...] = src[0, :, a:b].astype(BF16)

    rows = master.shape[1]
    return pl.pallas_call(
        body,
        out_shape=[shape((rows, b - a), BF16) for a, b in spans],
        in_specs=[VMEM],
        out_specs=[VMEM] * len(spans),
        cost_estimate=cost(0, master.size * 6),
        compiler_params=SMALL,
        name="round_head",
    )(master)


def frame_scales(frame_mask, segment_ids):
    micro, frames = frame_mask.shape

    def body(mask, ids, out):
        for m in range(micro):
            valid = mask[m : m + 1, :].astype(F32)
            own = ids[m : m + 1, :]
            per_frame = jnp.zeros_like(valid)
            for s in range(SEGS):
                hit = (own == s).astype(F32)
                per_frame += hit * jnp.sum(hit * valid, axis=1, keepdims=True)
            scale = valid / jnp.maximum(per_frame, 1.0)
            out[m * frames : (m + 1) * frames, :] = jnp.broadcast_to(scale, (LANES, frames)).T

    return pl.pallas_call(
        body,
        out_shape=shape((micro * frames, LANES), F32),
        in_specs=[VMEM, VMEM],
        out_specs=VMEM,
        cost_estimate=cost(0, micro * frames * LANES * 4),
        compiler_params=SMALL,
        name="frame_scales",
    )(frame_mask, segment_ids)


def transposed(x):
    rows, columns = x.shape
    tile = next(t for t in (640, 512, 384, 256, 128) if columns % t == 0)

    def body(src, out):
        for at in range(0, columns, tile):
            out[at : at + tile, :] = src[:, at : at + tile].T

    return pl.pallas_call(
        body,
        out_shape=shape((columns, rows), x.dtype),
        in_specs=[VMEM],
        out_specs=VMEM,
        compiler_params=SMALL,
        cost_estimate=cost(0, x.size * 4),
        name="transposed",
    )(x)


def logits_of(frames_all, blocks, owner, tile=512):
    tokens, features = frames_all.shape
    rows, classes = blocks[0].shape
    tile = min(tile, tokens)

    def body(x, *refs):
        parts, (kept, logits, sent, head, sem) = refs[: len(blocks)], refs[len(blocks) :]
        for k, part in enumerate(parts):
            at = pl.multiple_of(owner(k) * rows, 16)
            head[pl.ds(at, rows), :] = part[...]
        keep = pltpu.make_async_copy(head, kept, sem)
        keep.start()
        for at in range(0, tokens, tile):
            value = jnp.dot(x[at : at + tile, :], head[...], preferred_element_type=F32)
            logits[at : at + tile, :] = value
            sent[at : at + tile, :] = value.astype(BF16)
        keep.wait()

    return pl.pallas_call(
        body,
        out_shape=[shape((features, classes), BF16), shape((tokens, classes), F32), shape((tokens, classes), BF16)],
        in_specs=[VMEM] * (1 + len(blocks)),
        out_specs=[pl.BlockSpec(memory_space=pltpu.HBM), VMEM, VMEM],
        scratch_shapes=[pltpu.VMEM((features, classes), BF16), pltpu.SemaphoreType.DMA],
        compiler_params=SMALL,
        cost_estimate=cost(2 * tokens * features * classes, tokens * features * 2),
        name="logits_of",
    )(frames_all, *blocks)


def gradient(partners, logits, candidates, scales, replicas):
    tokens, classes = logits.shape
    micro, chips = partners.shape[0], replicas // 2
    frames = tokens // micro

    def body(partners_ref, logits_ref, scale_ref, *refs):
        options, out = refs[:-1], refs[-1]
        mine = lax.axis_index("rep")
        for m in range(micro):
            here = slice(m * frames, (m + 1) * frames)
            wanted = partners_ref[m, mine]
            back = (mine // 2 - wanted // 2 + chips) % chips
            choice = jnp.where(wanted % 2 == mine % 2, back - 1, back + chips - 1)
            for k, option in enumerate(options):

                @pl.when(choice == k)
                def _(option=option, here=here):
                    for a in range(0, classes, LANES):
                        b = min(a + LANES, classes)
                        gap = logits_ref[here, a:b] - option[here, a:b].astype(F32)
                        out[here, a:b] = (gap * scale_ref[here, : b - a]).astype(BF16)

    return pl.pallas_call(
        body,
        out_shape=shape((tokens, classes), BF16),
        in_specs=[SMEM] + [VMEM] * (2 + len(candidates)),
        out_specs=VMEM,
        compiler_params=SMALL,
        cost_estimate=cost(3 * tokens * classes, tokens * classes * 8),
        name="gradient",
    )(partners, logits, scales, *candidates)


def head_terms(turned, grad, owner, places, rows):
    tokens, classes = grad.shape

    def body(turned_ref, grad_ref, *outs):
        for k, out in zip(places, outs):
            at = pl.multiple_of(owner(k) * rows, 16)
            term = jnp.dot(turned_ref[pl.ds(at, rows), :], grad_ref[...], preferred_element_type=F32)
            out[...] = term.astype(BF16)

    return pl.pallas_call(
        body,
        out_shape=[shape((rows, classes), BF16)] * len(places),
        in_specs=[VMEM, VMEM],
        out_specs=[VMEM] * len(places),
        compiler_params=SMALL,
        cost_estimate=cost(2 * tokens * rows * classes * len(places), len(places) * rows * tokens * 2),
        name="head_terms",
    )(turned, grad)


def hidden_gradient(grads, heads, tile=256):
    tokens, features = grads[0].shape[0], heads[0].shape[0]
    count = len(grads)

    def body(*refs):
        out = refs[-1]
        total = None
        for g, h in zip(refs[:count], refs[count:-1]):
            term = lax.dot_general(g[...], h[...], (((1,), (1,)), ((), ())), preferred_element_type=F32)
            total = term if total is None else total + term
        out[...] = total.astype(BF16)

    classes = sum(g.shape[1] for g in grads)
    return pl.pallas_call(
        body,
        out_shape=shape((tokens, features), BF16),
        grid=(tokens // tile,),
        in_specs=[pl.BlockSpec((tile, g.shape[1]), lambda i: (i, 0)) for g in grads]
        + [pl.BlockSpec(h.shape, lambda i: (0, 0)) for h in heads],
        out_specs=pl.BlockSpec((tile, features), lambda i: (i, 0)),
        cost_estimate=cost(2 * tokens * features * classes, tokens * features * 2),
        compiler_params=SMALL,
        name="hidden_gradient",
    )(*grads, *heads)


def adam(sums, spans, master, moment_one, moment_two):
    each = len(sums[0])
    flat = [x for group in sums for x in group]

    def body(*refs):
        terms, (w, one, two, new_w, new_one, new_two) = refs[: len(flat)], refs[len(flat) :]
        for i, (a, b) in enumerate(spans):
            g = sum(t[...].astype(F32) for t in terms[i * each : (i + 1) * each])
            first = 0.9 * one[0, :, a:b] + 0.1 * g
            second = 0.99 * two[0, :, a:b] + 0.01 * g * g
            new_one[0, :, a:b] = first
            new_two[0, :, a:b] = second
            new_w[0, :, a:b] = w[0, :, a:b] - 0.01 * first / (jnp.sqrt(second) + 1e-08)

    out = shape(master.shape, F32)
    return pl.pallas_call(
        body,
        out_shape=[out, out, out],
        in_specs=[VMEM] * (len(flat) + 3),
        out_specs=[VMEM] * 3,
        cost_estimate=cost(12 * master.size, 24 * master.size),
        compiler_params=SMALL,
        name="adam",
    )(*flat, master, moment_one, moment_two)


def across_replicas(sent, replicas):
    chips = replicas // 2
    swap = [(r, r ^ 1) for r in range(replicas)]
    far, near = [], []
    for s in range(1, chips):
        far.append(lax.ppermute(sent, "rep", [(r, (r + 2 * s) % replicas) for r in range(replicas)]))
    for x in [sent] + far:
        near.append(lax.ppermute(x, "rep", swap))
    return far + near


def step(replicas, shards, hidden, partners, frame_mask, segment_ids, master, moment_one, moment_two):
    micro, _, frames, features = hidden.shape
    rows, classes = master.shape[1], master.shape[2]
    aligned = rows % 16 == 0
    ring = Ring("dp", shards)
    frames_all = hidden.reshape(micro * frames, features)
    cut = 2 * LANES
    spans = [(a, min(a + cut, classes)) for a in range(0, classes, cut)]

    scales = frame_scales(frame_mask, segment_ids)
    turned = transposed(frames_all)
    low = round_head(master, spans)
    heads, grads, sums = [], [], []
    gathered = [ring.gather(x, i % 2 == 0) for i, x in enumerate(low)]
    for i, blocks in enumerate(gathered):
        longer = i % 2 == 0
        if aligned:
            head, logits, sent = logits_of(frames_all, blocks, ring.owner)
        else:
            whole = jnp.zeros((features, blocks[0].shape[1]), BF16)
            for k, block in enumerate(blocks):
                whole = lax.dynamic_update_slice(whole, block, (ring.owner(k) * rows, 0))
            head, logits, sent = logits_of(frames_all, [whole], lambda k: 0)
        others = across_replicas(sent, replicas)
        grad = gradient(partners, logits, others, scales, replicas)
        ups, downs = ring.steps(longer)
        first = sorted({ups, shards - downs})
        rest = [k for k in range(shards) if k not in first]
        if aligned:
            found = dict(zip(first, head_terms(turned, grad, ring.owner, first, rows)))
            found.update(zip(rest, head_terms(turned, grad, ring.owner, rest, rows)))
        else:
            product = jnp.dot(turned, grad, preferred_element_type=F32).astype(BF16)
            found = {
                k: lax.dynamic_slice(product, (ring.owner(k) * rows, 0), (rows, grad.shape[1])) for k in range(shards)
            }
        heads.append(head)
        grads.append(grad)
        sums.append(ring.scatter_sum([found[k] for k in range(shards)], longer))
    hidden_grad = hidden_gradient(grads, heads).reshape(hidden.shape)
    return (hidden_grad, *adam(sums, spans, master, moment_one, moment_two))


def solution(mesh):
    whole = P("rep", "dp", None)
    replicas, shards = mesh.shape["rep"], mesh.shape["dp"]

    def program(*args):
        return step(replicas, shards, *args)

    return jax.shard_map(
        program,
        mesh=mesh,
        in_specs=(P(None, "rep", "dp", None), P(), P(None, "dp"), P(None, "dp"), whole, whole, whole),
        out_specs=(P(None, "rep", "dp", None), whole, whole, whole),
        check_vma=False,
    )
```

time: 191 us -> 86.2 us (0.45)
  waiting for transfers between devices: 145 us -> 33.6 us
  starting transfers between devices: 0.12 us -> 33.4 us
  matrix products: 16.7 us -> 0 us
  Pallas kernels: 0 us -> 14.6 us
  between operations: 13.9 us -> 0.91 us
  local copies, waits for them, and re-layouts: 9.33 us -> 3.17 us
  other arithmetic: 6.23 us -> 0.32 us
    all_gather x2 -> x0, waiting for transfers between devices: 84.6 us -> none  [the longest x1 52.2 us: per_device(): head_full = lax.all_gather(head_low, 'dp', axis=1, tiled=True)[0]]
    unnamed x4 -> x0, waiting for transfers between devices: 60.3 us -> none
    ppermute x0 -> x34, waiting for transfers between devices: none -> 33.6 us  [the longest x2 15.8 us: across_replicas(): lax.ppermute(sent, 'rep', [(r, (r + 2 * s) % replicas) for r in range(rep...]
    ppermute x0 -> x34, starting transfers between devices: none -> 33.4 us  [the longest x14 21.9 us: send_up(): return lax.ppermute(x, self.axis, self.up)]
    dot_general x3 -> x0, matrix products: 16.7 us -> none  [the longest x1 6.04 us: per_device(): logits = jnp.dot(frames_all, head_full, preferred_element_type=jnp.float32)]
    pallas_call x0 -> x13, Pallas kernels: none -> 14.6 us  [the longest x1 4.12 us: hidden_gradient(): pl.pallas_call(body, out_shape=shape((tokens, features), BF16), grid=(tok...]
    unnamed x22 -> x16, local copies, waits for them, and re-layouts: 7.82 us -> 3.17 us
    dot_general x1 -> x0, other arithmetic: 3.4 us -> none  [per_device(): jnp.einsum('km,kmtv->mtv', selector, piece, preferred_element_type=jnp.fl...]
  transfers between devices with their start and end apart: 3 -> 34, of which waited for: 3 -> 12; matrix products, arithmetic and copies ran while one was open for 4% -> 0% of each run, Pallas kernels for 0% -> 15%
where the time goes in v1:
time: 86.2 us; the launch traced here: 86 us
  waiting for transfers between devices  33.6 us (39%)
  starting transfers between devices  33.4 us (39%)
  Pallas kernels  14.6 us (17%)
  local copies, waits for them, and re-layouts  3.17 us (4%)
  between operations  0.91 us (1%)
    ppermute x14, starting transfers between devices, send_up(): return lax.ppermute(x, self.axis, self.up)  21.9 us
    ppermute x2, waiting for transfers between devices, across_replicas(): lax.ppermute(sent, 'rep', [(r, (r + 2 * s) % replicas) for r in range(rep...  15.8 us
    ppermute x14, waiting for transfers between devices, send_up(): return lax.ppermute(x, self.axis, self.up)  12.8 us
    ppermute x14, starting transfers between devices, send_down(): return lax.ppermute(x, self.axis, self.down)  8.82 us
    ppermute x14, waiting for transfers between devices, send_down(): return lax.ppermute(x, self.axis, self.down)  5.01 us
    pallas_call x1, Pallas kernels, hidden_gradient(): pl.pallas_call(body, out_shape=shape((tokens, features), BF16), grid=(tok...  4.12 us
    pallas_call x2, Pallas kernels, logits_of(): pl.pallas_call(body, out_shape=[shape((features, classes), BF16), shape((...  3.38 us
    unnamed x16, local copies, waits for them, and re-layouts  3.17 us
  transfers between devices with their start and end apart: 34, of which 12 were waited for; matrix products, arithmetic and copies ran while one was open for 0% of the time, Pallas kernels for 15%

profile of v1, /device:TPU:0, one launch (start us, length us, event | category | flops | bytes accessed | tf_op | source)
XLA Modules:
  0.0 86.0 jit_solution(14416853400268059614)
XLA Ops:
  1.7 3.1 %collective-permute-start.3 = (bf16[240,256]{1,0:T(8,128)(2,1)S(1)}, bf16[240,256]{1,0:T(8,128)(2,1)S(1)}, u32[]{:S(2)}, u32[]{:S(2)}) collective-permute-start(bf16[240,256]{1,0:T(8,128)(2,1)S(1)} %get-tuple-element.31.refs_0_), channel_id=1, source_target_pairs={{0,2},{2,4},{4,6},{6,7},{7,5},{5,3},{3,1},{1,0},{8,10},{10,12},{12... | collective-permute-start | bytes 368648 | tf_op jit(solution)/shard_map/ppermute | solution.py:43
  4.8 3.3 %collective-permute-done.3.refs_7_ = bf16[240,256]{1,0:T(8,128)(2,1)S(1)} collective-permute-done((bf16[240,256]{1,0:T(8,128)(2,1)S(1)}, bf16[240,256]{1,0:T(8,128)(2,1)S(1)}, u32[]{:S(2)}, u32[]{:S(2)}) %collective-permute-start.3) | collective-permute-done | bytes 122912 | tf_op jit(solution)/shard_map/ppermute | solution.py:43
  8.1 1.8 %collective-permute-start.4 = (bf16[240,256]{1,0:T(8,128)(2,1)S(1)}, bf16[240,256]{1,0:T(8,128)(2,1)S(1)}, u32[]{:S(2)}, u32[]{:S(2)}) collective-permute-start(bf16[240,256]{1,0:T(8,128)(2,1)S(1)} %collective-permute-done.3.refs_7_), channel_id=1, source_target_pairs={{0,2},{2,4},{4,6},{6,7},{7,5},{5,3},{3,1},{1,0},{8,10},{10,12},{12... | collective-permute-start | bytes 368648 | tf_op jit(solution)/shard_map/ppermute | solution.py:43
  10.1 1.7 %collective-permute-start.1 = (bf16[240,256]{1,0:T(8,128)(2,1)S(1)}, bf16[240,256]{1,0:T(8,128)(2,1)S(1)}, u32[]{:S(2)}, u32[]{:S(2)}) collective-permute-start(bf16[240,256]{1,0:T(8,128)(2,1)S(1)} %collective-permute-done.refs_1_), channel_id=1, source_target_pairs={{2,0},{4,2},{6,4},{7,6},{5,7},{3,5},{1,3},{0,1},{10,8},{12,10},{14... | collective-permute-start | bytes 368648 | tf_op jit(solution)/shard_map/ppermute | solution.py:46
  12.9 1.8 %collective-permute-start.5 = (bf16[240,256]{1,0:T(8,128)(2,1)S(1)}, bf16[240,256]{1,0:T(8,128)(2,1)S(1)}, u32[]{:S(2)}, u32[]{:S(2)}) collective-permute-start(bf16[240,256]{1,0:T(8,128)(2,1)S(1)} %collective-permute-done.4.refs_6_), channel_id=1, source_target_pairs={{0,2},{2,4},{4,6},{6,7},{7,5},{5,3},{3,1},{1,0},{8,10},{10,12},{12... | collective-permute-start | bytes 368648 | tf_op jit(solution)/shard_map/ppermute | solution.py:43
  14.7 1.6 %collective-permute-start.14 = (bf16[240,244]{1,0:T(8,128)(2,1)S(1)}, bf16[240,244]{1,0:T(8,128)(2,1)S(1)}, u32[]{:S(2)}, u32[]{:S(2)}) collective-permute-start(bf16[240,244]{1,0:T(8,128)(2,1)S(1)} %get-tuple-element.34.refs_0_), channel_id=1, source_target_pairs={{0,2},{2,4},{4,6},{6,7},{7,5},{5,3},{3,1},{1,0},{8,10},{10,12},{12... | collective-permute-start | bytes 351368 | tf_op jit(solution)/shard_map/ppermute | solution.py:43
  16.8 3.5 %collective-permute-done.14.refs_7_ = bf16[240,244]{1,0:T(8,128)(2,1)S(1)} collective-permute-done((bf16[240,244]{1,0:T(8,128)(2,1)S(1)}, bf16[240,244]{1,0:T(8,128)(2,1)S(1)}, u32[]{:S(2)}, u32[]{:S(2)}) %collective-permute-start.14) | collective-permute-done | bytes 117152 | tf_op jit(solution)/shard_map/ppermute | solution.py:43
  20.3 1.6 %collective-permute-start.15 = (bf16[240,244]{1,0:T(8,128)(2,1)S(1)}, bf16[240,244]{1,0:T(8,128)(2,1)S(1)}, u32[]{:S(2)}, u32[]{:S(2)}) collective-permute-start(bf16[240,244]{1,0:T(8,128)(2,1)S(1)} %collective-permute-done.14.refs_7_), channel_id=1, source_target_pairs={{0,2},{2,4},{4,6},{6,7},{7,5},{5,3},{3,1},{1,0},{8,10},{10,12},{12... | collective-permute-start | bytes 351368 | tf_op jit(solution)/shard_map/ppermute | solution.py:43
  24.6 1.7 %collective-permute-done.15.refs_6_ = bf16[240,244]{1,0:T(8,128)(2,1)S(1)} collective-permute-done((bf16[240,244]{1,0:T(8,128)(2,1)S(1)}, bf16[240,244]{1,0:T(8,128)(2,1)S(1)}, u32[]{:S(2)}, u32[]{:S(2)}) %collective-permute-start.15) | collective-permute-done | bytes 117152 | tf_op jit(solution)/shard_map/ppermute | solution.py:43
  26.3 1.6 %collective-permute-start.16 = (bf16[240,244]{1,0:T(8,128)(2,1)S(1)}, bf16[240,244]{1,0:T(8,128)(2,1)S(1)}, u32[]{:S(2)}, u32[]{:S(2)}) collective-permute-start(bf16[240,244]{1,0:T(8,128)(2,1)S(1)} %collective-permute-done.15.refs_6_), channel_id=1, source_target_pairs={{0,2},{2,4},{4,6},{6,7},{7,5},{5,3},{3,1},{1,0},{8,10},{10,12},{12... | collective-permute-start | bytes 351368 | tf_op jit(solution)/shard_map/ppermute | solution.py:43
  28.9 2.1 %copy-done = bf16[2,1,512,1920]{3,2,1,0:T(8,128)(2,1)S(1)} copy-done((bf16[2,1,512,1920]{3,2,1,0:T(8,128)(2,1)S(1)}, bf16[2,1,512,1920]{3,2,1,0:T(8,128)(2,1)}, u32[]{:S(2)}) %copy-start) | copy-done | bytes 3932184
  31.0 1.7 %logits_of.2 = (bf16[1920,256]{1,0:T(8,128)(2,1)S(1)}, f32[1024,256]{1,0:T(8,128)S(1)}, bf16[1024,256]{1,0:T(8,128)(2,1)S(1)}) custom-call(bf16[1024,1920]{1,0:T(8,128)(2,1)S(1)} %bitcast.4, bf16[240,256]{1,0:T(8,128)(2,1)S(1)} %get-tuple-element.31.refs_0_, bf16[240,256]{1,0:T(8,128)(2,1)S(1)} %collective-permute-done.refs_1_, ...), custom_call_target="tpu_custom_call" | custom-call | flops 1006632960 | bytes 3932160 | tf_op jit(solution)/shard_map/logits_of/pallas_call | solution.py:153
  32.7 1.6 %collective-permute-start.7 = (bf16[1024,256]{1,0:T(8,128)(2,1)S(1)}, bf16[1024,256]{1,0:T(8,128)(2,1)S(1)}, u32[]{:S(2)}, u32[]{:S(2)}) collective-permute-start(bf16[1024,256]{1,0:T(8,128)(2,1)S(1)} %get-tuple-element.33), channel_id=1, source_target_pairs={{0,16},{8,24},{16,0},{24,8},{1,17},{9,25},{17,1},{25,9},{2,18},{10... | collective-permute-start | bytes 1572872 | tf_op jit(solution)/shard_map/ppermute | solution.py:275
  34.3 1.7 %logits_of.3 = (bf16[1920,244]{1,0:T(8,128)(2,1)S(1)}, f32[1024,244]{1,0:T(8,128)S(1)}, bf16[1024,244]{1,0:T(8,128)(2,1)S(1)}) custom-call(bf16[1024,1920]{1,0:T(8,128)(2,1)S(1)} %bitcast.5, bf16[240,244]{1,0:T(8,128)(2,1)S(1)} %get-tuple-element.34.refs_0_, bf16[240,244]{1,0:T(8,128)(2,1)S(1)} %collective-permute-done.10.refs_1_, ...), custom_call_target="tpu_custom_call" | custom-call | flops 959447040 | bytes 3932160 | tf_op jit(solution)/shard_map/logits_of/pallas_call | solution.py:153
  36.6 10.7 %collective-permute-done.7.refs_0_ = bf16[1024,256]{1,0:T(8,128)(2,1)S(1)} collective-permute-done((bf16[1024,256]{1,0:T(8,128)(2,1)S(1)}, bf16[1024,256]{1,0:T(8,128)(2,1)S(1)}, u32[]{:S(2)}, u32[]{:S(2)}) %collective-permute-start.7) | collective-permute-done | bytes 524320 | tf_op jit(solution)/shard_map/ppermute | solution.py:275
  47.8 5.1 %collective-permute-done.17.refs_0_ = bf16[1024,244]{1,0:T(8,128)(2,1)S(1)} collective-permute-done((bf16[1024,244]{1,0:T(8,128)(2,1)S(1)}, bf16[1024,244]{1,0:T(8,128)(2,1)S(1)}, u32[]{:S(2)}, u32[]{:S(2)}) %collective-permute-start.17) | collective-permute-done | bytes 499744 | tf_op jit(solution)/shard_map/ppermute | solution.py:275
  55.6 1.3 %collective-permute-start.20 = (bf16[240,256]{1,0:T(8,128)(2,1)S(1)}, bf16[240,256]{1,0:T(8,128)(2,1)S(1)}, u32[]{:S(2)}, u32[]{:S(2)}) collective-permute-start(bf16[240,256]{1,0:T(8,128)(2,1)S(1)} %get-tuple-element.43), channel_id=1, source_target_pairs={{0,2},{2,4},{4,6},{6,7},{7,5},{5,3},{3,1},{1,0},{8,10},{10,12},{12... | collective-permute-start | bytes 368648 | tf_op jit(solution)/shard_map/ppermute | solution.py:43
  58.1 1.6 %collective-permute-start.27 = (bf16[240,244]{1,0:T(8,128)(2,1)S(1)}, bf16[240,244]{1,0:T(8,128)(2,1)S(1)}, u32[]{:S(2)}, u32[]{:S(2)}) collective-permute-start(bf16[240,244]{1,0:T(8,128)(2,1)S(1)} %get-tuple-element.50), channel_id=1, source_target_pairs={{0,2},{2,4},{4,6},{6,7},{7,5},{5,3},{3,1},{1,0},{8,10},{10,12},{12... | collective-permute-start | bytes 351368 | tf_op jit(solution)/shard_map/ppermute | solution.py:43
  64.3 1.6 %collective-permute-done.30 = bf16[240,244]{1,0:T(8,128)(2,1)S(1)} collective-permute-done((bf16[240,244]{1,0:T(8,128)(2,1)S(1)}, bf16[240,244]{1,0:T(8,128)(2,1)S(1)}, u32[]{:S(2)}, u32[]{:S(2)}) %collective-permute-start.30) | collective-permute-done | bytes 117152 | tf_op jit(solution)/shard_map/ppermute | solution.py:46
  66.5 1.9 %collective-permute-done.24 = bf16[240,256]{1,0:T(8,128)(2,1)S(1)} collective-permute-done((bf16[240,256]{1,0:T(8,128)(2,1)S(1)}, bf16[240,256]{1,0:T(8,128)(2,1)S(1)}, u32[]{:S(2)}, u32[]{:S(2)}) %collective-permute-start.24) | collective-permute-done | bytes 122912 | tf_op jit(solution)/shard_map/ppermute | solution.py:46
  69.0 1.6 %collective-permute-start.22 = (bf16[240,256]{1,0:T(8,128)(2,1)S(1)}, bf16[240,256]{1,0:T(8,128)(2,1)S(1)}, u32[]{:S(2)}, u32[]{:S(2)}) collective-permute-start(bf16[240,256]{1,0:T(8,128)(2,1)S(1)} %add.31), channel_id=1, source_target_pairs={{0,2},{2,4},{4,6},{6,7},{7,5},{5,3},{3,1},{1,0},{8,10},{10,12},{12... | collective-permute-start | bytes 368648 | tf_op jit(solution)/shard_map/ppermute | solution.py:43
  72.8 3.3 %collective-permute-done.28 = bf16[240,244]{1,0:T(8,128)(2,1)S(1)} collective-permute-done((bf16[240,244]{1,0:T(8,128)(2,1)S(1)}, bf16[240,244]{1,0:T(8,128)(2,1)S(1)}, u32[]{:S(2)}, u32[]{:S(2)}) %collective-permute-start.28) | collective-permute-done | bytes 117152 | tf_op jit(solution)/shard_map/ppermute | solution.py:43
  78.7 1.8 %collective-permute-start.23 = (bf16[240,256]{1,0:T(8,128)(2,1)S(1)}, bf16[240,256]{1,0:T(8,128)(2,1)S(1)}, u32[]{:S(2)}, u32[]{:S(2)}) collective-permute-start(bf16[240,256]{1,0:T(8,128)(2,1)S(1)} %add.32), channel_id=1, source_target_pairs={{0,2},{2,4},{4,6},{6,7},{7,5},{5,3},{3,1},{1,0},{8,10},{10,12},{12... | collective-permute-start | bytes 368648 | tf_op jit(solution)/shard_map/ppermute | solution.py:43
  80.5 4.1 %hidden_gradient.1 = bf16[1024,1920]{1,0:T(8,128)(2,1)} custom-call(bf16[1024,256]{1,0:T(8,128)(2,1)S(1)} %gradient.2.refs_0_.grad_ref, bf16[1024,244]{1,0:T(8,128)(2,1)S(1)} %gradient.3.refs_1_.grad_ref, bf16[1920,256]{1,0:T(8,128)(2,1)S(1)} %get-tuple-element.37.refs_2_, bf16[1920,244]{1,0:T(8,128)(2,1)S(1)} %get-tuple-element.38.refs_3_), custom_call_target="tpu_custom_call" | custom-call | flops 1966080000 | bytes 3932160 | tf_op jit(solution)/shard_map/hidden_gradient/pallas_call | solution.py:231
  (83 shorter events, 23.4 us)
Async XLA Ops:
  1.7 6.4 %collective-permute-start.3 = (bf16[240,256]{1,0:T(8,128)(2,1)S(1)}, bf16[240,256]{1,0:T(8,128)(2,1)S(1)}, u32[]{:S(2)}, u32[]{:S(2)}) collective-permute-start(bf16[240,256]{1,0:T(8,128)(2,1)S(1)} %get-tuple-element.31.refs_0_), channel_id=1, source_target_pairs={{0,2},{2,4},{4,6},{6,7},{7,5},{5,3},{3,1},{1,0},{8,10},{10,12},{12... | collective-permute-start | bytes 368648 | tf_op jit(solution)/shard_map/ppermute | solution.py:43
  9.9 6.5 %collective-permute-start.10 = (bf16[240,244]{1,0:T(8,128)(2,1)S(1)}, bf16[240,244]{1,0:T(8,128)(2,1)S(1)}, u32[]{:S(2)}, u32[]{:S(2)}) collective-permute-start(bf16[240,244]{1,0:T(8,128)(2,1)S(1)} %get-tuple-element.34.refs_0_), channel_id=1, source_target_pairs={{2,0},{4,2},{6,4},{7,6},{5,7},{3,5},{1,3},{0,1},{10,8},{12,10},{14... | collective-permute-start | bytes 351368 | tf_op jit(solution)/shard_map/ppermute | solution.py:46
  10.1 12.5 %collective-permute-start.1 = (bf16[240,256]{1,0:T(8,128)(2,1)S(1)}, bf16[240,256]{1,0:T(8,128)(2,1)S(1)}, u32[]{:S(2)}, u32[]{:S(2)}) collective-permute-start(bf16[240,256]{1,0:T(8,128)(2,1)S(1)} %collective-permute-done.refs_1_), channel_id=1, source_target_pairs={{2,0},{4,2},{6,4},{7,6},{5,7},{3,5},{1,3},{0,1},{10,8},{12,10},{14... | collective-permute-start | bytes 368648 | tf_op jit(solution)/shard_map/ppermute | solution.py:46
  12.9 10.6 %collective-permute-start.5 = (bf16[240,256]{1,0:T(8,128)(2,1)S(1)}, bf16[240,256]{1,0:T(8,128)(2,1)S(1)}, u32[]{:S(2)}, u32[]{:S(2)}) collective-permute-start(bf16[240,256]{1,0:T(8,128)(2,1)S(1)} %collective-permute-done.4.refs_6_), channel_id=1, source_target_pairs={{0,2},{2,4},{4,6},{6,7},{7,5},{5,3},{3,1},{1,0},{8,10},{10,12},{12... | collective-permute-start | bytes 368648 | tf_op jit(solution)/shard_map/ppermute | solution.py:43
  22.6 6.3 %collective-permute-start.2 = (bf16[240,256]{1,0:T(8,128)(2,1)S(1)}, bf16[240,256]{1,0:T(8,128)(2,1)S(1)}, u32[]{:S(2)}, u32[]{:S(2)}) collective-permute-start(bf16[240,256]{1,0:T(8,128)(2,1)S(1)} %collective-permute-done.1.refs_2_), channel_id=1, source_target_pairs={{2,0},{4,2},{6,4},{7,6},{5,7},{3,5},{1,3},{0,1},{10,8},{12,10},{14... | collective-permute-start | bytes 368648 | tf_op jit(solution)/shard_map/ppermute | solution.py:46
  26.3 8.0 %collective-permute-start.16 = (bf16[240,244]{1,0:T(8,128)(2,1)S(1)}, bf16[240,244]{1,0:T(8,128)(2,1)S(1)}, u32[]{:S(2)}, u32[]{:S(2)}) collective-permute-start(bf16[240,244]{1,0:T(8,128)(2,1)S(1)} %collective-permute-done.15.refs_6_), channel_id=1, source_target_pairs={{0,2},{2,4},{4,6},{6,7},{7,5},{5,3},{3,1},{1,0},{8,10},{10,12},{12... | collective-permute-start | bytes 351368 | tf_op jit(solution)/shard_map/ppermute | solution.py:43
  27.9 6.4 %collective-permute-start.13 = (bf16[240,244]{1,0:T(8,128)(2,1)S(1)}, bf16[240,244]{1,0:T(8,128)(2,1)S(1)}, u32[]{:S(2)}, u32[]{:S(2)}) collective-permute-start(bf16[240,244]{1,0:T(8,128)(2,1)S(1)} %collective-permute-done.12.refs_3_), channel_id=1, source_target_pairs={{2,0},{4,2},{6,4},{7,6},{5,7},{3,5},{1,3},{0,1},{10,8},{12,10},{14... | collective-permute-start | bytes 351368 | tf_op jit(solution)/shard_map/ppermute | solution.py:46
  32.7 14.6 %collective-permute-start.7 = (bf16[1024,256]{1,0:T(8,128)(2,1)S(1)}, bf16[1024,256]{1,0:T(8,128)(2,1)S(1)}, u32[]{:S(2)}, u32[]{:S(2)}) collective-permute-start(bf16[1024,256]{1,0:T(8,128)(2,1)S(1)} %get-tuple-element.33), channel_id=1, source_target_pairs={{0,16},{8,24},{16,0},{24,8},{1,17},{9,25},{17,1},{25,9},{2,18},{10... | collective-permute-start | bytes 1572872 | tf_op jit(solution)/shard_map/ppermute | solution.py:275
  36.0 16.9 %collective-permute-start.17 = (bf16[1024,244]{1,0:T(8,128)(2,1)S(1)}, bf16[1024,244]{1,0:T(8,128)(2,1)S(1)}, u32[]{:S(2)}, u32[]{:S(2)}) collective-permute-start(bf16[1024,244]{1,0:T(8,128)(2,1)S(1)} %get-tuple-element.36), channel_id=1, source_target_pairs={{0,16},{8,24},{16,0},{24,8},{1,17},{9,25},{17,1},{25,9},{2,18},{10... | collective-permute-start | bytes 1499144 | tf_op jit(solution)/shard_map/ppermute | solution.py:275
  36.6 17.8 %collective-permute-start.8 = (bf16[1024,256]{1,0:T(8,128)(2,1)S(1)}, bf16[1024,256]{1,0:T(8,128)(2,1)S(1)}, u32[]{:S(2)}, u32[]{:S(2)}) collective-permute-start(bf16[1024,256]{1,0:T(8,128)(2,1)S(1)} %get-tuple-element.33), channel_id=1, source_target_pairs={{0,8},{8,0},{16,24},{24,16},{1,9},{9,1},{17,25},{25,17},{2,10},{10... | collective-permute-start | bytes 1572872 | tf_op jit(solution)/shard_map/ppermute | solution.py:277
  47.3 7.1 %collective-permute-start.9 = (bf16[1024,256]{1,0:T(8,128)(2,1)S(1)}, bf16[1024,256]{1,0:T(8,128)(2,1)S(1)}, u32[]{:S(2)}, u32[]{:S(2)}) collective-permute-start(bf16[1024,256]{1,0:T(8,128)(2,1)S(1)} %collective-permute-done.7.refs_0_), channel_id=1, source_target_pairs={{0,8},{8,0},{16,24},{24,16},{1,9},{9,1},{17,25},{25,17},{2,10},{10... | collective-permute-start | bytes 1572872 | tf_op jit(solution)/shard_map/ppermute | solution.py:277
  47.3 9.7 %collective-permute-start.18 = (bf16[1024,244]{1,0:T(8,128)(2,1)S(1)}, bf16[1024,244]{1,0:T(8,128)(2,1)S(1)}, u32[]{:S(2)}, u32[]{:S(2)}) collective-permute-start(bf16[1024,244]{1,0:T(8,128)(2,1)S(1)} %get-tuple-element.36), channel_id=1, source_target_pairs={{0,8},{8,0},{16,24},{24,16},{1,9},{9,1},{17,25},{25,17},{2,10},{10... | collective-permute-start | bytes 1499144 | tf_op jit(solution)/shard_map/ppermute | solution.py:277
  55.6 6.3 %collective-permute-start.20 = (bf16[240,256]{1,0:T(8,128)(2,1)S(1)}, bf16[240,256]{1,0:T(8,128)(2,1)S(1)}, u32[]{:S(2)}, u32[]{:S(2)}) collective-permute-start(bf16[240,256]{1,0:T(8,128)(2,1)S(1)} %get-tuple-element.43), channel_id=1, source_target_pairs={{0,2},{2,4},{4,6},{6,7},{7,5},{5,3},{3,1},{1,0},{8,10},{10,12},{12... | collective-permute-start | bytes 368648 | tf_op jit(solution)/shard_map/ppermute | solution.py:43
  58.1 12.5 %collective-permute-start.27 = (bf16[240,244]{1,0:T(8,128)(2,1)S(1)}, bf16[240,244]{1,0:T(8,128)(2,1)S(1)}, u32[]{:S(2)}, u32[]{:S(2)}) collective-permute-start(bf16[240,244]{1,0:T(8,128)(2,1)S(1)} %get-tuple-element.50), channel_id=1, source_target_pairs={{0,2},{2,4},{4,6},{6,7},{7,5},{5,3},{3,1},{1,0},{8,10},{10,12},{12... | collective-permute-start | bytes 351368 | tf_op jit(solution)/shard_map/ppermute | solution.py:43
  59.7 6.2 %collective-permute-start.30 = (bf16[240,244]{1,0:T(8,128)(2,1)S(1)}, bf16[240,244]{1,0:T(8,128)(2,1)S(1)}, u32[]{:S(2)}, u32[]{:S(2)}) collective-permute-start(bf16[240,244]{1,0:T(8,128)(2,1)S(1)} %get-tuple-element.54), channel_id=1, source_target_pairs={{2,0},{4,2},{6,4},{7,6},{5,7},{3,5},{1,3},{0,1},{10,8},{12,10},{14... | collective-permute-start | bytes 351368 | tf_op jit(solution)/shard_map/ppermute | solution.py:46
  60.2 8.2 %collective-permute-start.24 = (bf16[240,256]{1,0:T(8,128)(2,1)S(1)}, bf16[240,256]{1,0:T(8,128)(2,1)S(1)}, u32[]{:S(2)}, u32[]{:S(2)}) collective-permute-start(bf16[240,256]{1,0:T(8,128)(2,1)S(1)} %get-tuple-element.46), channel_id=1, source_target_pairs={{2,0},{4,2},{6,4},{7,6},{5,7},{3,5},{1,3},{0,1},{10,8},{12,10},{14... | collective-permute-start | bytes 368648 | tf_op jit(solution)/shard_map/ppermute | solution.py:46
  62.0 7.0 %collective-permute-start.21 = (bf16[240,256]{1,0:T(8,128)(2,1)S(1)}, bf16[240,256]{1,0:T(8,128)(2,1)S(1)}, u32[]{:S(2)}, u32[]{:S(2)}) collective-permute-start(bf16[240,256]{1,0:T(8,128)(2,1)S(1)} %add.30), channel_id=1, source_target_pairs={{0,2},{2,4},{4,6},{6,7},{7,5},{5,3},{3,1},{1,0},{8,10},{10,12},{12... | collective-permute-start | bytes 368648 | tf_op jit(solution)/shard_map/ppermute | solution.py:43
  65.9 6.2 %collective-permute-start.31 = (bf16[240,244]{1,0:T(8,128)(2,1)S(1)}, bf16[240,244]{1,0:T(8,128)(2,1)S(1)}, u32[]{:S(2)}, u32[]{:S(2)}) collective-permute-start(bf16[240,244]{1,0:T(8,128)(2,1)S(1)} %add.37), channel_id=1, source_target_pairs={{2,0},{4,2},{6,4},{7,6},{5,7},{3,5},{1,3},{0,1},{10,8},{12,10},{14... | collective-permute-start | bytes 351368 | tf_op jit(solution)/shard_map/ppermute | solution.py:46
  68.4 8.7 %collective-permute-start.25 = (bf16[240,256]{1,0:T(8,128)(2,1)S(1)}, bf16[240,256]{1,0:T(8,128)(2,1)S(1)}, u32[]{:S(2)}, u32[]{:S(2)}) collective-permute-start(bf16[240,256]{1,0:T(8,128)(2,1)S(1)} %add.33), channel_id=1, source_target_pairs={{2,0},{4,2},{6,4},{7,6},{5,7},{3,5},{1,3},{0,1},{10,8},{12,10},{14... | collective-permute-start | bytes 368648 | tf_op jit(solution)/shard_map/ppermute | solution.py:46
  69.0 9.7 %collective-permute-start.22 = (bf16[240,256]{1,0:T(8,128)(2,1)S(1)}, bf16[240,256]{1,0:T(8,128)(2,1)S(1)}, u32[]{:S(2)}, u32[]{:S(2)}) collective-permute-start(bf16[240,256]{1,0:T(8,128)(2,1)S(1)} %add.31), channel_id=1, source_target_pairs={{0,2},{2,4},{4,6},{6,7},{7,5},{5,3},{3,1},{1,0},{8,10},{10,12},{12... | collective-permute-start | bytes 368648 | tf_op jit(solution)/shard_map/ppermute | solution.py:43
  72.2 6.1 %collective-permute-start.32 = (bf16[240,244]{1,0:T(8,128)(2,1)S(1)}, bf16[240,244]{1,0:T(8,128)(2,1)S(1)}, u32[]{:S(2)}, u32[]{:S(2)}) collective-permute-start(bf16[240,244]{1,0:T(8,128)(2,1)S(1)} %add.38), channel_id=1, source_target_pairs={{2,0},{4,2},{6,4},{7,6},{5,7},{3,5},{1,3},{0,1},{10,8},{12,10},{14... | collective-permute-start | bytes 351368 | tf_op jit(solution)/shard_map/ppermute | solution.py:46
  76.1 8.5 %collective-permute-start.29 = (bf16[240,244]{1,0:T(8,128)(2,1)S(1)}, bf16[240,244]{1,0:T(8,128)(2,1)S(1)}, u32[]{:S(2)}, u32[]{:S(2)}) collective-permute-start(bf16[240,244]{1,0:T(8,128)(2,1)S(1)} %add.36), channel_id=1, source_target_pairs={{0,2},{2,4},{4,6},{6,7},{7,5},{5,3},{3,1},{1,0},{8,10},{10,12},{12... | collective-permute-start | bytes 351368 | tf_op jit(solution)/shard_map/ppermute | solution.py:43
  77.2 7.5 %collective-permute-start.26 = (bf16[240,256]{1,0:T(8,128)(2,1)S(1)}, bf16[240,256]{1,0:T(8,128)(2,1)S(1)}, u32[]{:S(2)}, u32[]{:S(2)}) collective-permute-start(bf16[240,256]{1,0:T(8,128)(2,1)S(1)} %add.34), channel_id=1, source_target_pairs={{2,0},{4,2},{6,4},{7,6},{5,7},{3,5},{1,3},{0,1},{10,8},{12,10},{14... | collective-permute-start | bytes 368648 | tf_op jit(solution)/shard_map/ppermute | solution.py:46
  78.4 6.3 %collective-permute-start.33 = (bf16[240,244]{1,0:T(8,128)(2,1)S(1)}, bf16[240,244]{1,0:T(8,128)(2,1)S(1)}, u32[]{:S(2)}, u32[]{:S(2)}) collective-permute-start(bf16[240,244]{1,0:T(8,128)(2,1)S(1)} %add.39), channel_id=1, source_target_pairs={{2,0},{4,2},{6,4},{7,6},{5,7},{3,5},{1,3},{0,1},{10,8},{12,10},{14... | collective-permute-start | bytes 351368 | tf_op jit(solution)/shard_map/ppermute | solution.py:46
  (18 other events, 130.9 us)

commit v2 on v1

--- a/solution.py
+++ b/solution.py
@@ -215,7 +215,7 @@
     )(turned, grad)
 
 
-def hidden_gradient(grads, heads, tile=256):
+def hidden_gradient(grads, heads, tile=512):
     tokens, features = grads[0].shape[0], heads[0].shape[0]
     count = len(grads)
 
@@ -241,30 +241,41 @@
     )(*grads, *heads)
 
 
-def adam(sums, spans, master, moment_one, moment_two):
-    each = len(sums[0])
-    flat = [x for group in sums for x in group]
+def adam(terms, span, master, moment_one, moment_two, before):
+    a, b = span
+    rows = master.shape[1]
+    count = len(terms)
 
     def body(*refs):
-        terms, (w, one, two, new_w, new_one, new_two) = refs[: len(flat)], refs[len(flat) :]
-        for i, (a, b) in enumerate(spans):
-            g = sum(t[...].astype(F32) for t in terms[i * each : (i + 1) * each])
-            first = 0.9 * one[0, :, a:b] + 0.1 * g
-            second = 0.99 * two[0, :, a:b] + 0.01 * g * g
-            new_one[0, :, a:b] = first
-            new_two[0, :, a:b] = second
-            new_w[0, :, a:b] = w[0, :, a:b] - 0.01 * first / (jnp.sqrt(second) + 1e-08)
-
-    out = shape(master.shape, F32)
-    return pl.pallas_call(
-        body,
-        out_shape=[out, out, out],
-        in_specs=[VMEM] * (len(flat) + 3),
-        out_specs=[VMEM] * 3,
-        cost_estimate=cost(12 * master.size, 24 * master.size),
+        parts, (w, one, two) = refs[:count], refs[count : count + 3]
+        outs, staged, sems = refs[-7:-4], refs[-4:-1], refs[-1]
+        g = sum(t[...].astype(F32) for t in parts)
+        first = 0.9 * one[0, :, a:b] + 0.1 * g
+        second = 0.99 * two[0, :, a:b] + 0.01 * g * g
+        copies = [
+            pltpu.make_async_copy(held, out.at[0, :, a:b], sems.at[i]) for i, (held, out) in enumerate(zip(staged, outs))
+        ]
+        staged[1][...] = first
+        copies[1].start()
+        staged[2][...] = second
+        copies[2].start()
+        staged[0][...] = w[0, :, a:b] - 0.01 * first / (jnp.sqrt(second) + 1e-08)
+        copies[0].start()
+        for copy in copies:
+            copy.wait()
+
+    hbm = pl.BlockSpec(memory_space=pltpu.HBM)
+    return pl.pallas_call(
+        body,
+        out_shape=[shape(master.shape, F32)] * 3,
+        in_specs=[VMEM] * (count + 3) + [hbm] * len(before),
+        out_specs=[hbm] * 3,
+        scratch_shapes=[pltpu.VMEM((rows, b - a), F32)] * 3 + [pltpu.SemaphoreType.DMA((3,))],
+        input_output_aliases={count + 3 + i: i for i in range(len(before))},
+        cost_estimate=cost(12 * rows * (b - a), 24 * rows * (b - a)),
         compiler_params=SMALL,
         name="adam",
-    )(*flat, master, moment_one, moment_two)
+    )(*terms, master, moment_one, moment_two, *before)
 
 
 def across_replicas(sent, replicas):
@@ -318,7 +329,10 @@
         grads.append(grad)
         sums.append(ring.scatter_sum([found[k] for k in range(shards)], longer))
     hidden_grad = hidden_gradient(grads, heads).reshape(hidden.shape)
-    return (hidden_grad, *adam(sums, spans, master, moment_one, moment_two))
+    new = ()
+    for i, span in enumerate(spans):
+        new = adam(sums[i], span, master, moment_one, moment_two, new)
+    return (hidden_grad, *new)
 
 
 def solution(mesh):

time: 86.2 us -> 86.6 us (level)
    pallas_call x1 -> x2, Pallas kernels: 1.32 us -> 1.99 us  [adam(): pl.pallas_call(body, out_shape=[shape(master.shape, F32)] * 3, in_specs=[...]
  transfers between devices with their start and end apart: 34 -> 34, of which waited for: 12 -> 12; matrix products, arithmetic and copies ran while one was open for 0% -> 0% of each run, Pallas kernels for 15% -> 16%
where the time goes in v2:
time: 86.6 us; the launch traced here: 86.4 us
  waiting for transfers between devices  33.6 us (39%)
  starting transfers between devices  33.4 us (39%)
  Pallas kernels  15 us (17%)
  local copies, waits for them, and re-layouts  3.17 us (4%)
  between operations  0.92 us (1%)
    ppermute x14, starting transfers between devices, send_up(): return lax.ppermute(x, self.axis, self.up)  21.9 us
    ppermute x2, waiting for transfers between devices, across_replicas(): lax.ppermute(sent, 'rep', [(r, (r + 2 * s) % replicas) for r in range(rep...  15.8 us
    ppermute x14, waiting for transfers between devices, send_up(): return lax.ppermute(x, self.axis, self.up)  12.8 us
    ppermute x14, starting transfers between devices, send_down(): return lax.ppermute(x, self.axis, self.down)  8.82 us
    ppermute x14, waiting for transfers between devices, send_down(): return lax.ppermute(x, self.axis, self.down)  5.01 us
    pallas_call x1, Pallas kernels, hidden_gradient(): pl.pallas_call(body, out_shape=shape((tokens, features), BF16), grid=(tok...  3.87 us
    pallas_call x2, Pallas kernels, logits_of(): pl.pallas_call(body, out_shape=[shape((features, classes), BF16), shape((...  3.38 us
    unnamed x16, local copies, waits for them, and re-layouts  3.17 us
  transfers between devices with their start and end apart: 34, of which 12 were waited for; matrix products, arithmetic and copies ran while one was open for 0% of the time, Pallas kernels for 16%

profile of v2, /device:TPU:0, one launch (start us, length us, event | category | flops | bytes accessed | tf_op | source)
XLA Modules:
  0.0 86.4 jit_solution(333369175497158909)
XLA Ops:
  1.7 3.1 %collective-permute-start.3 = (bf16[240,256]{1,0:T(8,128)(2,1)S(1)}, bf16[240,256]{1,0:T(8,128)(2,1)S(1)}, u32[]{:S(2)}, u32[]{:S(2)}) collective-permute-start(bf16[240,256]{1,0:T(8,128)(2,1)S(1)} %get-tuple-element.34.refs_0_), channel_id=1, source_target_pairs={{0,2},{2,4},{4,6},{6,7},{7,5},{5,3},{3,1},{1,0},{8,10},{10,12},{12... | collective-permute-start | bytes 368648 | tf_op jit(solution)/shard_map/ppermute | solution.py:43
  4.8 3.3 %collective-permute-done.3.refs_7_ = bf16[240,256]{1,0:T(8,128)(2,1)S(1)} collective-permute-done((bf16[240,256]{1,0:T(8,128)(2,1)S(1)}, bf16[240,256]{1,0:T(8,128)(2,1)S(1)}, u32[]{:S(2)}, u32[]{:S(2)}) %collective-permute-start.3) | collective-permute-done | bytes 122912 | tf_op jit(solution)/shard_map/ppermute | solution.py:43
  8.1 1.8 %collective-permute-start.4 = (bf16[240,256]{1,0:T(8,128)(2,1)S(1)}, bf16[240,256]{1,0:T(8,128)(2,1)S(1)}, u32[]{:S(2)}, u32[]{:S(2)}) collective-permute-start(bf16[240,256]{1,0:T(8,128)(2,1)S(1)} %collective-permute-done.3.refs_7_), channel_id=1, source_target_pairs={{0,2},{2,4},{4,6},{6,7},{7,5},{5,3},{3,1},{1,0},{8,10},{10,12},{12... | collective-permute-start | bytes 368648 | tf_op jit(solution)/shard_map/ppermute | solution.py:43
  10.1 1.7 %collective-permute-start.1 = (bf16[240,256]{1,0:T(8,128)(2,1)S(1)}, bf16[240,256]{1,0:T(8,128)(2,1)S(1)}, u32[]{:S(2)}, u32[]{:S(2)}) collective-permute-start(bf16[240,256]{1,0:T(8,128)(2,1)S(1)} %collective-permute-done.refs_1_), channel_id=1, source_target_pairs={{2,0},{4,2},{6,4},{7,6},{5,7},{3,5},{1,3},{0,1},{10,8},{12,10},{14... | collective-permute-start | bytes 368648 | tf_op jit(solution)/shard_map/ppermute | solution.py:46
  12.9 1.8 %collective-permute-start.5 = (bf16[240,256]{1,0:T(8,128)(2,1)S(1)}, bf16[240,256]{1,0:T(8,128)(2,1)S(1)}, u32[]{:S(2)}, u32[]{:S(2)}) collective-permute-start(bf16[240,256]{1,0:T(8,128)(2,1)S(1)} %collective-permute-done.4.refs_6_), channel_id=1, source_target_pairs={{0,2},{2,4},{4,6},{6,7},{7,5},{5,3},{3,1},{1,0},{8,10},{10,12},{12... | collective-permute-start | bytes 368648 | tf_op jit(solution)/shard_map/ppermute | solution.py:43
  14.7 1.6 %collective-permute-start.14 = (bf16[240,244]{1,0:T(8,128)(2,1)S(1)}, bf16[240,244]{1,0:T(8,128)(2,1)S(1)}, u32[]{:S(2)}, u32[]{:S(2)}) collective-permute-start(bf16[240,244]{1,0:T(8,128)(2,1)S(1)} %get-tuple-element.37.refs_0_), channel_id=1, source_target_pairs={{0,2},{2,4},{4,6},{6,7},{7,5},{5,3},{3,1},{1,0},{8,10},{10,12},{12... | collective-permute-start | bytes 351368 | tf_op jit(solution)/shard_map/ppermute | solution.py:43
  16.8 3.5 %collective-permute-done.14.refs_7_ = bf16[240,244]{1,0:T(8,128)(2,1)S(1)} collective-permute-done((bf16[240,244]{1,0:T(8,128)(2,1)S(1)}, bf16[240,244]{1,0:T(8,128)(2,1)S(1)}, u32[]{:S(2)}, u32[]{:S(2)}) %collective-permute-start.14) | collective-permute-done | bytes 117152 | tf_op jit(solution)/shard_map/ppermute | solution.py:43
  20.3 1.6 %collective-permute-start.15 = (bf16[240,244]{1,0:T(8,128)(2,1)S(1)}, bf16[240,244]{1,0:T(8,128)(2,1)S(1)}, u32[]{:S(2)}, u32[]{:S(2)}) collective-permute-start(bf16[240,244]{1,0:T(8,128)(2,1)S(1)} %collective-permute-done.14.refs_7_), channel_id=1, source_target_pairs={{0,2},{2,4},{4,6},{6,7},{7,5},{5,3},{3,1},{1,0},{8,10},{10,12},{12... | collective-permute-start | bytes 351368 | tf_op jit(solution)/shard_map/ppermute | solution.py:43
  24.6 1.7 %collective-permute-done.15.refs_6_ = bf16[240,244]{1,0:T(8,128)(2,1)S(1)} collective-permute-done((bf16[240,244]{1,0:T(8,128)(2,1)S(1)}, bf16[240,244]{1,0:T(8,128)(2,1)S(1)}, u32[]{:S(2)}, u32[]{:S(2)}) %collective-permute-start.15) | collective-permute-done | bytes 117152 | tf_op jit(solution)/shard_map/ppermute | solution.py:43
  26.3 1.6 %collective-permute-start.16 = (bf16[240,244]{1,0:T(8,128)(2,1)S(1)}, bf16[240,244]{1,0:T(8,128)(2,1)S(1)}, u32[]{:S(2)}, u32[]{:S(2)}) collective-permute-start(bf16[240,244]{1,0:T(8,128)(2,1)S(1)} %collective-permute-done.15.refs_6_), channel_id=1, source_target_pairs={{0,2},{2,4},{4,6},{6,7},{7,5},{5,3},{3,1},{1,0},{8,10},{10,12},{12... | collective-permute-start | bytes 351368 | tf_op jit(solution)/shard_map/ppermute | solution.py:43
  28.9 2.1 %copy-done = bf16[2,1,512,1920]{3,2,1,0:T(8,128)(2,1)S(1)} copy-done((bf16[2,1,512,1920]{3,2,1,0:T(8,128)(2,1)S(1)}, bf16[2,1,512,1920]{3,2,1,0:T(8,128)(2,1)}, u32[]{:S(2)}) %copy-start) | copy-done | bytes 3932184
  31.0 1.7 %logits_of.2 = (bf16[1920,256]{1,0:T(8,128)(2,1)S(1)}, f32[1024,256]{1,0:T(8,128)S(1)}, bf16[1024,256]{1,0:T(8,128)(2,1)S(1)}) custom-call(bf16[1024,1920]{1,0:T(8,128)(2,1)S(1)} %bitcast.4, bf16[240,256]{1,0:T(8,128)(2,1)S(1)} %get-tuple-element.34.refs_0_, bf16[240,256]{1,0:T(8,128)(2,1)S(1)} %collective-permute-done.refs_1_, ...), custom_call_target="tpu_custom_call" | custom-call | flops 1006632960 | bytes 3932160 | tf_op jit(solution)/shard_map/logits_of/pallas_call | solution.py:153
  32.7 1.6 %collective-permute-start.7 = (bf16[1024,256]{1,0:T(8,128)(2,1)S(1)}, bf16[1024,256]{1,0:T(8,128)(2,1)S(1)}, u32[]{:S(2)}, u32[]{:S(2)}) collective-permute-start(bf16[1024,256]{1,0:T(8,128)(2,1)S(1)} %get-tuple-element.36), channel_id=1, source_target_pairs={{0,16},{8,24},{16,0},{24,8},{1,17},{9,25},{17,1},{25,9},{2,18},{10... | collective-permute-start | bytes 1572872 | tf_op jit(solution)/shard_map/ppermute | solution.py:286
  34.3 1.7 %logits_of.3 = (bf16[1920,244]{1,0:T(8,128)(2,1)S(1)}, f32[1024,244]{1,0:T(8,128)S(1)}, bf16[1024,244]{1,0:T(8,128)(2,1)S(1)}) custom-call(bf16[1024,1920]{1,0:T(8,128)(2,1)S(1)} %bitcast.5, bf16[240,244]{1,0:T(8,128)(2,1)S(1)} %get-tuple-element.37.refs_0_, bf16[240,244]{1,0:T(8,128)(2,1)S(1)} %collective-permute-done.10.refs_1_, ...), custom_call_target="tpu_custom_call" | custom-call | flops 959447040 | bytes 3932160 | tf_op jit(solution)/shard_map/logits_of/pallas_call | solution.py:153
  36.6 10.7 %collective-permute-done.7.refs_0_ = bf16[1024,256]{1,0:T(8,128)(2,1)S(1)} collective-permute-done((bf16[1024,256]{1,0:T(8,128)(2,1)S(1)}, bf16[1024,256]{1,0:T(8,128)(2,1)S(1)}, u32[]{:S(2)}, u32[]{:S(2)}) %collective-permute-start.7) | collective-permute-done | bytes 524320 | tf_op jit(solution)/shard_map/ppermute | solution.py:286
  47.8 5.1 %collective-permute-done.17.refs_0_ = bf16[1024,244]{1,0:T(8,128)(2,1)S(1)} collective-permute-done((bf16[1024,244]{1,0:T(8,128)(2,1)S(1)}, bf16[1024,244]{1,0:T(8,128)(2,1)S(1)}, u32[]{:S(2)}, u32[]{:S(2)}) %collective-permute-start.17) | collective-permute-done | bytes 499744 | tf_op jit(solution)/shard_map/ppermute | solution.py:286
  55.6 1.3 %collective-permute-start.27 = (bf16[240,256]{1,0:T(8,128)(2,1)S(1)}, bf16[240,256]{1,0:T(8,128)(2,1)S(1)}, u32[]{:S(2)}, u32[]{:S(2)}) collective-permute-start(bf16[240,256]{1,0:T(8,128)(2,1)S(1)} %get-tuple-element.54), channel_id=1, source_target_pairs={{0,2},{2,4},{4,6},{6,7},{7,5},{5,3},{3,1},{1,0},{8,10},{10,12},{12... | collective-permute-start | bytes 368648 | tf_op jit(solution)/shard_map/ppermute | solution.py:43
  58.1 1.6 %collective-permute-start.20 = (bf16[240,244]{1,0:T(8,128)(2,1)S(1)}, bf16[240,244]{1,0:T(8,128)(2,1)S(1)}, u32[]{:S(2)}, u32[]{:S(2)}) collective-permute-start(bf16[240,244]{1,0:T(8,128)(2,1)S(1)} %get-tuple-element.45), channel_id=1, source_target_pairs={{0,2},{2,4},{4,6},{6,7},{7,5},{5,3},{3,1},{1,0},{8,10},{10,12},{12... | collective-permute-start | bytes 351368 | tf_op jit(solution)/shard_map/ppermute | solution.py:43
  64.3 1.6 %collective-permute-done.23 = bf16[240,244]{1,0:T(8,128)(2,1)S(1)} collective-permute-done((bf16[240,244]{1,0:T(8,128)(2,1)S(1)}, bf16[240,244]{1,0:T(8,128)(2,1)S(1)}, u32[]{:S(2)}, u32[]{:S(2)}) %collective-permute-start.23) | collective-permute-done | bytes 117152 | tf_op jit(solution)/shard_map/ppermute | solution.py:46
  66.5 1.9 %collective-permute-done.31 = bf16[240,256]{1,0:T(8,128)(2,1)S(1)} collective-permute-done((bf16[240,256]{1,0:T(8,128)(2,1)S(1)}, bf16[240,256]{1,0:T(8,128)(2,1)S(1)}, u32[]{:S(2)}, u32[]{:S(2)}) %collective-permute-start.31) | collective-permute-done | bytes 122912 | tf_op jit(solution)/shard_map/ppermute | solution.py:46
  69.0 1.6 %collective-permute-start.29 = (bf16[240,256]{1,0:T(8,128)(2,1)S(1)}, bf16[240,256]{1,0:T(8,128)(2,1)S(1)}, u32[]{:S(2)}, u32[]{:S(2)}) collective-permute-start(bf16[240,256]{1,0:T(8,128)(2,1)S(1)} %add.36), channel_id=1, source_target_pairs={{0,2},{2,4},{4,6},{6,7},{7,5},{5,3},{3,1},{1,0},{8,10},{10,12},{12... | collective-permute-start | bytes 368648 | tf_op jit(solution)/shard_map/ppermute | solution.py:43
  72.8 3.3 %collective-permute-done.21 = bf16[240,244]{1,0:T(8,128)(2,1)S(1)} collective-permute-done((bf16[240,244]{1,0:T(8,128)(2,1)S(1)}, bf16[240,244]{1,0:T(8,128)(2,1)S(1)}, u32[]{:S(2)}, u32[]{:S(2)}) %collective-permute-start.21) | collective-permute-done | bytes 117152 | tf_op jit(solution)/shard_map/ppermute | solution.py:43
  78.7 1.8 %collective-permute-start.30 = (bf16[240,256]{1,0:T(8,128)(2,1)S(1)}, bf16[240,256]{1,0:T(8,128)(2,1)S(1)}, u32[]{:S(2)}, u32[]{:S(2)}) collective-permute-start(bf16[240,256]{1,0:T(8,128)(2,1)S(1)} %add.37), channel_id=1, source_target_pairs={{0,2},{2,4},{4,6},{6,7},{7,5},{5,3},{3,1},{1,0},{8,10},{10,12},{12... | collective-permute-start | bytes 368648 | tf_op jit(solution)/shard_map/ppermute | solution.py:43
  80.5 3.9 %hidden_gradient.1 = bf16[1024,1920]{1,0:T(8,128)(2,1)} custom-call(bf16[1024,256]{1,0:T(8,128)(2,1)S(1)} %gradient.2.refs_0_.grad_ref, bf16[1024,244]{1,0:T(8,128)(2,1)S(1)} %gradient.3.refs_1_.grad_ref, bf16[1920,256]{1,0:T(8,128)(2,1)S(1)} %get-tuple-element.40.refs_2_, bf16[1920,244]{1,0:T(8,128)(2,1)S(1)} %get-tuple-element.41.refs_3_), custom_call_target="tpu_custom_call" | custom-call | flops 1966080000 | bytes 3932160 | tf_op jit(solution)/shard_map/hidden_gradient/pallas_call | solution.py:231
  (84 shorter events, 24.1 us)
Async XLA Ops:
  1.7 6.4 %collective-permute-start.3 = (bf16[240,256]{1,0:T(8,128)(2,1)S(1)}, bf16[240,256]{1,0:T(8,128)(2,1)S(1)}, u32[]{:S(2)}, u32[]{:S(2)}) collective-permute-start(bf16[240,256]{1,0:T(8,128)(2,1)S(1)} %get-tuple-element.34.refs_0_), channel_id=1, source_target_pairs={{0,2},{2,4},{4,6},{6,7},{7,5},{5,3},{3,1},{1,0},{8,10},{10,12},{12... | collective-permute-start | bytes 368648 | tf_op jit(solution)/shard_map/ppermute | solution.py:43
  9.9 6.5 %collective-permute-start.10 = (bf16[240,244]{1,0:T(8,128)(2,1)S(1)}, bf16[240,244]{1,0:T(8,128)(2,1)S(1)}, u32[]{:S(2)}, u32[]{:S(2)}) collective-permute-start(bf16[240,244]{1,0:T(8,128)(2,1)S(1)} %get-tuple-element.37.refs_0_), channel_id=1, source_target_pairs={{2,0},{4,2},{6,4},{7,6},{5,7},{3,5},{1,3},{0,1},{10,8},{12,10},{14... | collective-permute-start | bytes 351368 | tf_op jit(solution)/shard_map/ppermute | solution.py:46
  10.1 12.5 %collective-permute-start.1 = (bf16[240,256]{1,0:T(8,128)(2,1)S(1)}, bf16[240,256]{1,0:T(8,128)(2,1)S(1)}, u32[]{:S(2)}, u32[]{:S(2)}) collective-permute-start(bf16[240,256]{1,0:T(8,128)(2,1)S(1)} %collective-permute-done.refs_1_), channel_id=1, source_target_pairs={{2,0},{4,2},{6,4},{7,6},{5,7},{3,5},{1,3},{0,1},{10,8},{12,10},{14... | collective-permute-start | bytes 368648 | tf_op jit(solution)/shard_map/ppermute | solution.py:46
  12.9 10.6 %collective-permute-start.5 = (bf16[240,256]{1,0:T(8,128)(2,1)S(1)}, bf16[240,256]{1,0:T(8,128)(2,1)S(1)}, u32[]{:S(2)}, u32[]{:S(2)}) collective-permute-start(bf16[240,256]{1,0:T(8,128)(2,1)S(1)} %collective-permute-done.4.refs_6_), channel_id=1, source_target_pairs={{0,2},{2,4},{4,6},{6,7},{7,5},{5,3},{3,1},{1,0},{8,10},{10,12},{12... | collective-permute-start | bytes 368648 | tf_op jit(solution)/shard_map/ppermute | solution.py:43
  22.6 6.3 %collective-permute-start.2 = (bf16[240,256]{1,0:T(8,128)(2,1)S(1)}, bf16[240,256]{1,0:T(8,128)(2,1)S(1)}, u32[]{:S(2)}, u32[]{:S(2)}) collective-permute-start(bf16[240,256]{1,0:T(8,128)(2,1)S(1)} %collective-permute-done.1.refs_2_), channel_id=1, source_target_pairs={{2,0},{4,2},{6,4},{7,6},{5,7},{3,5},{1,3},{0,1},{10,8},{12,10},{14... | collective-permute-start | bytes 368648 | tf_op jit(solution)/shard_map/ppermute | solution.py:46
  26.3 8.0 %collective-permute-start.16 = (bf16[240,244]{1,0:T(8,128)(2,1)S(1)}, bf16[240,244]{1,0:T(8,128)(2,1)S(1)}, u32[]{:S(2)}, u32[]{:S(2)}) collective-permute-start(bf16[240,244]{1,0:T(8,128)(2,1)S(1)} %collective-permute-done.15.refs_6_), channel_id=1, source_target_pairs={{0,2},{2,4},{4,6},{6,7},{7,5},{5,3},{3,1},{1,0},{8,10},{10,12},{12... | collective-permute-start | bytes 351368 | tf_op jit(solution)/shard_map/ppermute | solution.py:43
  27.9 6.4 %collective-permute-start.13 = (bf16[240,244]{1,0:T(8,128)(2,1)S(1)}, bf16[240,244]{1,0:T(8,128)(2,1)S(1)}, u32[]{:S(2)}, u32[]{:S(2)}) collective-permute-start(bf16[240,244]{1,0:T(8,128)(2,1)S(1)} %collective-permute-done.12.refs_3_), channel_id=1, source_target_pairs={{2,0},{4,2},{6,4},{7,6},{5,7},{3,5},{1,3},{0,1},{10,8},{12,10},{14... | collective-permute-start | bytes 351368 | tf_op jit(solution)/shard_map/ppermute | solution.py:46
  32.7 14.6 %collective-permute-start.7 = (bf16[1024,256]{1,0:T(8,128)(2,1)S(1)}, bf16[1024,256]{1,0:T(8,128)(2,1)S(1)}, u32[]{:S(2)}, u32[]{:S(2)}) collective-permute-start(bf16[1024,256]{1,0:T(8,128)(2,1)S(1)} %get-tuple-element.36), channel_id=1, source_target_pairs={{0,16},{8,24},{16,0},{24,8},{1,17},{9,25},{17,1},{25,9},{2,18},{10... | collective-permute-start | bytes 1572872 | tf_op jit(solution)/shard_map/ppermute | solution.py:286
  36.0 16.9 %collective-permute-start.17 = (bf16[1024,244]{1,0:T(8,128)(2,1)S(1)}, bf16[1024,244]{1,0:T(8,128)(2,1)S(1)}, u32[]{:S(2)}, u32[]{:S(2)}) collective-permute-start(bf16[1024,244]{1,0:T(8,128)(2,1)S(1)} %get-tuple-element.39), channel_id=1, source_target_pairs={{0,16},{8,24},{16,0},{24,8},{1,17},{9,25},{17,1},{25,9},{2,18},{10... | collective-permute-start | bytes 1499144 | tf_op jit(solution)/shard_map/ppermute | solution.py:286
  36.6 17.8 %collective-permute-start.8 = (bf16[1024,256]{1,0:T(8,128)(2,1)S(1)}, bf16[1024,256]{1,0:T(8,128)(2,1)S(1)}, u32[]{:S(2)}, u32[]{:S(2)}) collective-permute-start(bf16[1024,256]{1,0:T(8,128)(2,1)S(1)} %get-tuple-element.36), channel_id=1, source_target_pairs={{0,8},{8,0},{16,24},{24,16},{1,9},{9,1},{17,25},{25,17},{2,10},{10... | collective-permute-start | bytes 1572872 | tf_op jit(solution)/shard_map/ppermute | solution.py:288
  47.3 7.1 %collective-permute-start.9 = (bf16[1024,256]{1,0:T(8,128)(2,1)S(1)}, bf16[1024,256]{1,0:T(8,128)(2,1)S(1)}, u32[]{:S(2)}, u32[]{:S(2)}) collective-permute-start(bf16[1024,256]{1,0:T(8,128)(2,1)S(1)} %collective-permute-done.7.refs_0_), channel_id=1, source_target_pairs={{0,8},{8,0},{16,24},{24,16},{1,9},{9,1},{17,25},{25,17},{2,10},{10... | collective-permute-start | bytes 1572872 | tf_op jit(solution)/shard_map/ppermute | solution.py:288
  47.3 9.7 %collective-permute-start.18 = (bf16[1024,244]{1,0:T(8,128)(2,1)S(1)}, bf16[1024,244]{1,0:T(8,128)(2,1)S(1)}, u32[]{:S(2)}, u32[]{:S(2)}) collective-permute-start(bf16[1024,244]{1,0:T(8,128)(2,1)S(1)} %get-tuple-element.39), channel_id=1, source_target_pairs={{0,8},{8,0},{16,24},{24,16},{1,9},{9,1},{17,25},{25,17},{2,10},{10... | collective-permute-start | bytes 1499144 | tf_op jit(solution)/shard_map/ppermute | solution.py:288
  55.6 6.3 %collective-permute-start.27 = (bf16[240,256]{1,0:T(8,128)(2,1)S(1)}, bf16[240,256]{1,0:T(8,128)(2,1)S(1)}, u32[]{:S(2)}, u32[]{:S(2)}) collective-permute-start(bf16[240,256]{1,0:T(8,128)(2,1)S(1)} %get-tuple-element.54), channel_id=1, source_target_pairs={{0,2},{2,4},{4,6},{6,7},{7,5},{5,3},{3,1},{1,0},{8,10},{10,12},{12... | collective-permute-start | bytes 368648 | tf_op jit(solution)/shard_map/ppermute | solution.py:43
  58.1 12.5 %collective-permute-start.20 = (bf16[240,244]{1,0:T(8,128)(2,1)S(1)}, bf16[240,244]{1,0:T(8,128)(2,1)S(1)}, u32[]{:S(2)}, u32[]{:S(2)}) collective-permute-start(bf16[240,244]{1,0:T(8,128)(2,1)S(1)} %get-tuple-element.45), channel_id=1, source_target_pairs={{0,2},{2,4},{4,6},{6,7},{7,5},{5,3},{3,1},{1,0},{8,10},{10,12},{12... | collective-permute-start | bytes 351368 | tf_op jit(solution)/shard_map/ppermute | solution.py:43
  59.7 6.2 %collective-permute-start.23 = (bf16[240,244]{1,0:T(8,128)(2,1)S(1)}, bf16[240,244]{1,0:T(8,128)(2,1)S(1)}, u32[]{:S(2)}, u32[]{:S(2)}) collective-permute-start(bf16[240,244]{1,0:T(8,128)(2,1)S(1)} %get-tuple-element.49), channel_id=1, source_target_pairs={{2,0},{4,2},{6,4},{7,6},{5,7},{3,5},{1,3},{0,1},{10,8},{12,10},{14... | collective-permute-start | bytes 351368 | tf_op jit(solution)/shard_map/ppermute | solution.py:46
  60.2 8.2 %collective-permute-start.31 = (bf16[240,256]{1,0:T(8,128)(2,1)S(1)}, bf16[240,256]{1,0:T(8,128)(2,1)S(1)}, u32[]{:S(2)}, u32[]{:S(2)}) collective-permute-start(bf16[240,256]{1,0:T(8,128)(2,1)S(1)} %get-tuple-element.57), channel_id=1, source_target_pairs={{2,0},{4,2},{6,4},{7,6},{5,7},{3,5},{1,3},{0,1},{10,8},{12,10},{14... | collective-permute-start | bytes 368648 | tf_op jit(solution)/shard_map/ppermute | solution.py:46
  62.0 7.0 %collective-permute-start.28 = (bf16[240,256]{1,0:T(8,128)(2,1)S(1)}, bf16[240,256]{1,0:T(8,128)(2,1)S(1)}, u32[]{:S(2)}, u32[]{:S(2)}) collective-permute-start(bf16[240,256]{1,0:T(8,128)(2,1)S(1)} %add.35), channel_id=1, source_target_pairs={{0,2},{2,4},{4,6},{6,7},{7,5},{5,3},{3,1},{1,0},{8,10},{10,12},{12... | collective-permute-start | bytes 368648 | tf_op jit(solution)/shard_map/ppermute | solution.py:43
  65.9 6.2 %collective-permute-start.24 = (bf16[240,244]{1,0:T(8,128)(2,1)S(1)}, bf16[240,244]{1,0:T(8,128)(2,1)S(1)}, u32[]{:S(2)}, u32[]{:S(2)}) collective-permute-start(bf16[240,244]{1,0:T(8,128)(2,1)S(1)} %add.32), channel_id=1, source_target_pairs={{2,0},{4,2},{6,4},{7,6},{5,7},{3,5},{1,3},{0,1},{10,8},{12,10},{14... | collective-permute-start | bytes 351368 | tf_op jit(solution)/shard_map/ppermute | solution.py:46
  68.4 8.7 %collective-permute-start.32 = (bf16[240,256]{1,0:T(8,128)(2,1)S(1)}, bf16[240,256]{1,0:T(8,128)(2,1)S(1)}, u32[]{:S(2)}, u32[]{:S(2)}) collective-permute-start(bf16[240,256]{1,0:T(8,128)(2,1)S(1)} %add.38), channel_id=1, source_target_pairs={{2,0},{4,2},{6,4},{7,6},{5,7},{3,5},{1,3},{0,1},{10,8},{12,10},{14... | collective-permute-start | bytes 368648 | tf_op jit(solution)/shard_map/ppermute | solution.py:46
  69.0 9.7 %collective-permute-start.29 = (bf16[240,256]{1,0:T(8,128)(2,1)S(1)}, bf16[240,256]{1,0:T(8,128)(2,1)S(1)}, u32[]{:S(2)}, u32[]{:S(2)}) collective-permute-start(bf16[240,256]{1,0:T(8,128)(2,1)S(1)} %add.36), channel_id=1, source_target_pairs={{0,2},{2,4},{4,6},{6,7},{7,5},{5,3},{3,1},{1,0},{8,10},{10,12},{12... | collective-permute-start | bytes 368648 | tf_op jit(solution)/shard_map/ppermute | solution.py:43
  72.2 6.1 %collective-permute-start.25 = (bf16[240,244]{1,0:T(8,128)(2,1)S(1)}, bf16[240,244]{1,0:T(8,128)(2,1)S(1)}, u32[]{:S(2)}, u32[]{:S(2)}) collective-permute-start(bf16[240,244]{1,0:T(8,128)(2,1)S(1)} %add.33), channel_id=1, source_target_pairs={{2,0},{4,2},{6,4},{7,6},{5,7},{3,5},{1,3},{0,1},{10,8},{12,10},{14... | collective-permute-start | bytes 351368 | tf_op jit(solution)/shard_map/ppermute | solution.py:46
  76.1 9.3 %collective-permute-start.22 = (bf16[240,244]{1,0:T(8,128)(2,1)S(1)}, bf16[240,244]{1,0:T(8,128)(2,1)S(1)}, u32[]{:S(2)}, u32[]{:S(2)}) collective-permute-start(bf16[240,244]{1,0:T(8,128)(2,1)S(1)} %add.31), channel_id=1, source_target_pairs={{0,2},{2,4},{4,6},{6,7},{7,5},{5,3},{3,1},{1,0},{8,10},{10,12},{12... | collective-permute-start | bytes 351368 | tf_op jit(solution)/shard_map/ppermute | solution.py:43
  77.2 7.2 %collective-permute-start.33 = (bf16[240,256]{1,0:T(8,128)(2,1)S(1)}, bf16[240,256]{1,0:T(8,128)(2,1)S(1)}, u32[]{:S(2)}, u32[]{:S(2)}) collective-permute-start(bf16[240,256]{1,0:T(8,128)(2,1)S(1)} %add.39), channel_id=1, source_target_pairs={{2,0},{4,2},{6,4},{7,6},{5,7},{3,5},{1,3},{0,1},{10,8},{12,10},{14... | collective-permute-start | bytes 368648 | tf_op jit(solution)/shard_map/ppermute | solution.py:46
  78.4 7.1 %collective-permute-start.26 = (bf16[240,244]{1,0:T(8,128)(2,1)S(1)}, bf16[240,244]{1,0:T(8,128)(2,1)S(1)}, u32[]{:S(2)}, u32[]{:S(2)}) collective-permute-start(bf16[240,244]{1,0:T(8,128)(2,1)S(1)} %add.34), channel_id=1, source_target_pairs={{2,0},{4,2},{6,4},{7,6},{5,7},{3,5},{1,3},{0,1},{10,8},{12,10},{14... | collective-permute-start | bytes 351368 | tf_op jit(solution)/shard_map/ppermute | solution.py:46
  (18 other events, 129.8 us)
